TPU v7x, 512 devices: a whole 4x8x8 slice. The times are simulated.
512 devices in a mesh: row: 128 (over y, z, core), col: 4 (over x).
Axes of the slice: x: 4, y: 8, z: 8, core: 2. Of those that a mesh axis runs over, the one named last changes fastest.
Arguments:
- feat_in: bfloat16 [4096, 256, 256], P('row', 'col'), may hold values from -6 to 6
- conv_weight: bfloat16 [2304, 256], P('col'), may hold values from -0.125 to 0.125
- conv_bias: float32 [256], replicated, may hold values from -4 to 4
- proj_weight: bfloat16 [256, 768], replicated, may hold values from -0.375 to 0.375
- qkv_weight: bfloat16 [768, 2304], P('row'), may hold values from -2 to 2
- tissue: int32 [2048, 128], P('row', 'col'), may hold values from 0 to 1, as said below
- phase: int32 [2048, 128], P('row', 'col'), may hold values from 0 to 3, as said below
Outputs:
- attended: bfloat16 [2048, 128, 768], P('row', 'col')
Inputs may be any that keep to these rules, and one draw needn't show every extreme that they name: Within each column strip, phase is the token column plus an offset drawn for each token row, modulo 4. In each device's block of tokens, every phase holds at least one tissue token.
All inputs are finite; a program needn't handle non-finite values.
Results may differ from a plain program's by a relative error of at most 0.0065.
Values may be sent and summed in bfloat16 or wider, within the bound.
A program may use at most 64 MiB of HBM per device.

v0:
```python
import jax
import jax.numpy as jnp
from jax import lax
from jax.sharding import PartitionSpec as P

HD = 64
DILATION_STEP = 4


def partner(array, axis, apart):
    return lax.ppermute(array, axis, [(i, i ^ 1 << apart) for i in range(lax.axis_size(axis))])


def shifted(array, axis, by):
    length = lax.axis_size(axis)
    pairs = [(i, i + by) for i in range(length) if 0 <= i + by < length]
    return lax.ppermute(array, axis, pairs)


def layer_norm(values):
    centred = values - jnp.mean(values, axis=-1, keepdims=True)
    spread_rows = jnp.mean(centred * centred, axis=-1, keepdims=True)
    return centred * lax.rsqrt(spread_rows + 1e-05)


def fold_rows(operand, piece):
    return jnp.dot(operand, piece, preferred_element_type=jnp.float32)


def split_pair(buffer, bit, mine):
    slots = buffer.shape[0]
    view = buffer.reshape((slots >> bit + 1, 2, 1 << bit) + buffer.shape[1:])
    keep = jnp.where(mine == 0, view[:, 0], view[:, 1])
    send = jnp.where(mine == 0, view[:, 1], view[:, 0])
    return (keep, send)


def join_pair(keep, got, mine, shape):
    first = jnp.where(mine == 0, keep, got)
    second = jnp.where(mine == 0, got, keep)
    return jnp.stack([first, second], axis=1).reshape(shape)


def route_sender(payload, flags):
    mine_index = lax.axis_index("row")
    for bit in range(flag_bits(flags)):
        mine = mine_index >> bit & 1
        keep_a, send_a = split_pair(payload, bit, mine)
        keep_b, send_b = split_pair(flags, bit, mine)
        got_a, got_b = partner((send_a, send_b), "row", bit)
        payload = join_pair(keep_a, got_a, mine, payload.shape)
        flags = join_pair(keep_b, got_b, mine, flags.shape)
    return (payload, flags)


def route_back(payload):
    mine_index = lax.axis_index("row")
    for bit in range(flag_bits(payload)):
        mine = mine_index >> bit & 1
        keep_a, send_a = split_pair(payload, bit, mine)
        got_a = partner(send_a, "row", bit)
        payload = join_pair(keep_a, got_a, mine, payload.shape)
    return payload


def flag_bits(buffer):
    return buffer.shape[0].bit_length() - 1


def attend(queries, keys_all, values_all, key_live, query_live):
    row_count = queries.shape[0]
    model_width = queries.shape[1]
    head_count = model_width // HD
    query_heads = queries.reshape(row_count, head_count, HD).transpose(1, 0, 2)
    key_heads = keys_all.reshape(keys_all.shape[0], head_count, HD).transpose(1, 0, 2)
    value_heads = values_all.reshape(values_all.shape[0], head_count, HD).transpose(1, 0, 2)
    allowed = (key_live > 0.5)[None, :]

    def one_head(operands):
        query_head, key_head, value_head = operands
        scores = jnp.einsum(
            "qd,kd->qk", query_head, key_head, preferred_element_type=jnp.float32
        ) * HD ** (-0.5)
        scores = jnp.where(allowed, scores, -1e30)
        top_score = jnp.max(scores, axis=1, keepdims=True)
        weights = jnp.where(allowed, jnp.exp(scores - top_score), 0.0)
        denominator = jnp.sum(weights, axis=1, keepdims=True)
        return (
            jnp.dot(weights.astype(jnp.bfloat16), value_head, preferred_element_type=jnp.float32)
            / denominator
        )

    stacked = lax.map(one_head, (query_heads, key_heads, value_heads))
    merged = stacked.transpose(1, 0, 2).reshape(row_count, model_width)
    return (merged * query_live.astype(jnp.float32)[:, None]).astype(jnp.bfloat16)


def local(feat_in, conv_weight, conv_bias, proj_weight, qkv_weight, tissue, phase):
    in_rows, in_cols, channels = feat_in.shape
    out_rows = in_rows // 2
    out_cols = in_cols // 2
    token_count = out_rows * out_cols
    band_count = lax.axis_size("row")
    owner_labels = 2 * DILATION_STEP
    capacity = token_count // owner_labels
    model_width = qkv_weight.shape[0] * band_count
    left_edge = shifted(feat_in[:, in_cols - 1 :, :], "col", 1)
    widened = jnp.concatenate([left_edge, feat_in], axis=1)
    upper_edge = shifted(widened[in_rows - 1 :], "row", 1)
    padded = jnp.concatenate([upper_edge, widened], axis=0)
    windows = []
    for row_tap in range(3):
        for col_tap in range(3):
            window = padded[
                row_tap : row_tap + in_rows - 1 : 2, col_tap : col_tap + in_cols - 1 : 2, :
            ]
            windows.append(window.reshape(token_count, channels))
    patches = jnp.concatenate(windows, axis=1)
    conv_sum = fold_rows(patches, lax.all_gather(conv_weight, "col", axis=0, tiled=True))
    features = jax.nn.gelu(conv_sum + conv_bias).astype(jnp.bfloat16)
    tokens_bf = layer_norm(
        jnp.dot(features, proj_weight, preferred_element_type=jnp.float32)
    ).astype(jnp.bfloat16)
    phase_labels = phase.reshape(token_count)
    indicator_matrix = (
        phase_labels[:, None] == jnp.arange(DILATION_STEP, dtype=jnp.int32)[None, :]
    ).astype(jnp.int32)
    ranking = jnp.sum(
        (jnp.cumsum(indicator_matrix, axis=0) - indicator_matrix) * indicator_matrix, axis=1
    )
    target = (2 * phase_labels + ranking // capacity) * capacity + ranking % capacity
    inverse = (
        jnp.zeros((token_count,), jnp.int32)
        .at[target]
        .set(jnp.arange(token_count, dtype=jnp.int32))
    )
    tissue_flag = tissue.reshape(token_count).astype(jnp.bfloat16)
    flag_out = tissue_flag[inverse].reshape(owner_labels, capacity)
    qkv_local = fold_rows(tokens_bf, lax.all_gather(qkv_weight, "row", axis=0, tiled=True)).astype(
        jnp.bfloat16
    )
    arrived, arrived_flag = route_sender(
        qkv_local[inverse].reshape(owner_labels, capacity, 3 * model_width), flag_out
    )
    arrived_qkv = arrived.reshape(token_count, 3 * model_width)
    query_flag = arrived_flag.reshape(token_count)
    keys_values = arrived_qkv[:, model_width:]
    partner_kv, partner_flag = partner((keys_values, query_flag), "row", 0)
    joined_kv = jnp.concatenate([keys_values, partner_kv], axis=0)
    key_flag = jnp.concatenate([query_flag, partner_flag], axis=0)
    attended_rows = attend(
        arrived_qkv[:, :model_width],
        joined_kv[:, :model_width],
        joined_kv[:, model_width:],
        key_flag,
        query_flag,
    )
    returned = route_back(attended_rows.reshape(owner_labels, capacity, model_width))
    outputs = returned.reshape(token_count, model_width)[target]
    return outputs.reshape(out_rows, out_cols, model_width)


def solution(mesh):
    in_specs = (
        P("row", "col", None),
        P("col", None),
        P(),
        P(),
        P("row", None),
        P("row", "col"),
        P("row", "col"),
    )
    out_specs = P("row", "col", None)
    return jax.shard_map(local, mesh=mesh, in_specs=in_specs, out_specs=out_specs, check_vma=False)
```

profile of v0, /device:TPU:1, one launch (start us, length us, event | category | flops | bytes accessed | tf_op | source)
XLA Modules:
  0.0 378.8 jit_solution(9001759087257412841)
XLA Ops:
  9.0 3.9 %collective-permute-start.4 = (bf16[32,1,256]{2,1,0:T(2,128)(2,1)S(1)}, bf16[32,1,256]{2,1,0:T(2,128)(2,1)S(1)}, u32[]{:S(2)}, u32[]{:S(2)}) collective-permute-start(bf16[32,1,256]{2,1,0:T(2,128)(2,1)S(1)} %slice.131), channel_id=1, source_target_pairs={{0,1},{1,2},{2,3},{4,5},{5,6},{6,7},{8,9},{9,10},{10,11},{12,13},{... | collective-permute-start | bytes 49160 | tf_op jit(solution)/shard_map/ppermute | solution.py:17
  17.0 2.4 scatter_custom_fusion
  19.5 8.8 %slice.137 = bf16[16,32,256]{2,1,0:T(8,128)(2,1)} slice(bf16[32,64,256]{2,1,0:T(8,128)(2,1)} %param.9), slice={[0:31:2], [0:63:2], [0:256:1]} | slice | bytes 524288 | tf_op jit(solution)/shard_map/slice | solution.py:114
  28.2 7.0 %slice.138 = bf16[16,32,256]{2,1,0:T(8,128)(2,1)S(1)} slice(bf16[32,64,256]{2,1,0:T(8,128)(2,1)} %param.9), slice={[0:31:2], [1:64:2], [0:256:1]} | slice | bytes 524288 | tf_op jit(solution)/shard_map/slice | solution.py:114
  36.9 4.8 %collective-permute-start.5 = (bf16[1,65,256]{2,1,0:T(8,128)(2,1)S(1)}, bf16[1,65,256]{2,1,0:T(8,128)(2,1)S(1)}, u32[]{:S(2)}, u32[]{:S(2)}) collective-permute-start(bf16[1,65,256]{2,1,0:T(8,128)(2,1)S(1)} %fusion.51), channel_id=1, source_target_pairs={{0,4},{4,8},{8,12},{12,16},{16,20},{20,24},{24,28},{28,32},{32,36}... | collective-permute-start | bytes 99848 | tf_op jit(solution)/shard_map/ppermute | solution.py:17
  42.4 5.0 %slice.136 = bf16[16,32,256]{2,1,0:T(8,128)(2,1)} slice(bf16[32,65,256]{2,1,0:T(8,128)(2,1)S(1)} %pad_maximum_fusion.2), slice={[0:31:2], [0:63:2], [0:256:1]} | slice | bytes 524288 | tf_op jit(solution)/shard_map/slice | solution.py:114
  47.5 5.0 %slice.139 = bf16[16,32,256]{2,1,0:T(8,128)(2,1)} slice(bf16[32,65,256]{2,1,0:T(8,128)(2,1)S(1)} %pad_maximum_fusion.2), slice={[1:32:2], [0:63:2], [0:256:1]} | slice | bytes 524288 | tf_op jit(solution)/shard_map/slice | solution.py:114
  53.2 5.1 %slice.133 = bf16[16,32,256]{2,1,0:T(8,128)(2,1)} slice(bf16[33,65,256]{2,1,0:T(8,128)(2,1)S(1)} %maximum_maximum_fusion), slice={[0:31:2], [0:63:2], [0:256:1]} | slice | bytes 524288 | tf_op jit(solution)/shard_map/slice | solution.py:114
  58.3 5.0 %slice.134 = bf16[16,32,256]{2,1,0:T(8,128)(2,1)} slice(bf16[33,65,256]{2,1,0:T(8,128)(2,1)S(1)} %maximum_maximum_fusion), slice={[0:31:2], [1:64:2], [0:256:1]} | slice | bytes 524288 | tf_op jit(solution)/shard_map/slice | solution.py:114
  64.0 1.8 constant_dynamic-update-slice_fusion.8
  65.7 1.7 constant_dynamic-update-slice_fusion.7
  72.8 3.5 fusion.67
  76.6 57.6 %all-gather.6.cloned.1.call-done = bf16[128,6,2304]{2,1,0:T(8,128)(2,1)} async-done(((bf16[1,6,2304]{2,1,0:T(8,128)(2,1)}), bf16[128,6,2304]{2,1,0:T(8,128)(2,1)}) %all-gather.6.cloned.1.call-update) | async-done | bytes 3538960 | tf_op jit(solution)/shard_map/all_gather | solution.py:139
  134.2 6.6 %reshape.571 = bf16[768,2304]{1,0:T(8,128)(2,1)} reshape(bf16[128,6,2304]{2,1,0:T(8,128)(2,1)} %all-gather.6.cloned.1.call-done) | data formatting | bytes 7077888
  140.9 4.5 %convolution_convert_fusion = bf16[512,2304]{1,0:T(8,128)(2,1)S(1)} fusion(bf16[768,2304]{1,0:T(8,128)(2,1)} %reshape.571, f32[512,768]{1,0:T(8,128)} %copy-done.4, f32[512]{0:T(512)S(1)} %add_rsqrt_fusion, f32[512]{0:T(512)S(1)} %broadcast_multiply_fusion.1), kind=kOutput, calls=%fused_computation.28 | convolution fusion | flops 1814298624 | bytes 7475200 | tf_op jit(solution)/shard_map/dot_general | solution.py:27
  145.4 3.4 gather_fusion.1
  148.8 2.9 fusion.23
  151.8 2.1 collective-permute-start.6
  153.9 2.9 collective-permute-done.6
  159.7 2.3 collective-permute-start.7
  162.0 27.2 %collective-permute-done.7 = bf16[2,2,64,2304]{3,2,1,0:T(8,128)(2,1)} collective-permute-done((bf16[2,2,64,2304]{3,2,1,0:T(8,128)(2,1)}, bf16[2,2,64,2304]{3,2,1,0:T(8,128)(2,1)}, u32[]{:S(2)}, u32[]{:S(2)}) %collective-permute-start.7) | collective-permute-done | bytes 1179680 | tf_op jit(solution)/shard_map/ppermute | solution.py:11
  192.1 3.3 collective-permute-start.8
  195.5 3.5 gather_fusion
  199.1 49.2 %collective-permute-done.8 = bf16[1,4,64,2304]{3,2,1,0:T(8,128)(2,1)} collective-permute-done((bf16[1,4,64,2304]{3,2,1,0:T(8,128)(2,1)}, bf16[1,4,64,2304]{3,2,1,0:T(8,128)(2,1)}, u32[]{:S(2)}, u32[]{:S(2)}) %collective-permute-start.8) | collective-permute-done | bytes 1179680 | tf_op jit(solution)/shard_map/ppermute | solution.py:11
  251.3 2.5 collective-permute-start.9
  253.8 1.9 collective-permute-start
  256.9 1.9 collective-permute-start.1
  258.8 2.4 collective-permute-done.1
  261.2 3.0 collective-permute-start.2
  264.3 2.2 collective-permute-done.2
  266.6 4.7 %collective-permute-start.3 = (bf16[512]{0:T(512)(128)(2,1)S(1)}, bf16[512]{0:T(512)(128)(2,1)S(1)}, u32[]{:S(2)}, u32[]{:S(2)}) collective-permute-start(bf16[512]{0:T(512)(128)(2,1)S(1)} %reshape_reshape.30), channel_id=1, source_target_pairs={{0,4},{4,0},{8,12},{12,8},{16,20},{20,16},{24,28},{28,24},{32,36},... | collective-permute-start | bytes 3080 | tf_op jit(solution)/shard_map/ppermute | solution.py:11
  273.1 2.0 pad_maximum_fusion.3
  275.2 1.7 copy.129
  277.6 41.7 %while.10 = (s32[]{:T(128)}, f32[12,512,64]{1,2,0:T(8,128)}, pred[1,1024]{1,0:T(4,128)(4,1)S(1)}, bf16[12,512,64]{1,2,0:T(8,128)(2,1)}, bf16[12,1024,64]{1,2,0:T...) while((s32[]{:T(128)}, f32[12,512,64]{1,2,0:T(8,128)}, ...), condition=%wide.region_9.10_spmd, body=%wide.region_6.9_spmd.sunk | while | flops 141065216 | bytes 6767702 | solution.py:93
  277.6 1.5 fusion.79
  284.6 1.5 fusion.79
  288.0 1.5 fusion.79
  291.5 1.5 fusion.79
  298.4 1.5 fusion.79
  319.2 3.6 reshape.533
  323.9 3.7 broadcast_select_fusion.1
  327.6 2.7 copy.135
  330.4 2.2 collective-permute-start.10
  334.4 1.9 collective-permute-start.11
  336.3 10.3 %collective-permute-done.11 = bf16[2,2,64,768]{3,2,1,0:T(8,128)(2,1)S(1)} collective-permute-done((bf16[2,2,64,768]{3,2,1,0:T(8,128)(2,1)S(1)}, bf16[2,2,64,768]{3,2,1,0:T(8,128)(2,1)S(1)}, u32[]{:S(2)}, u32[]{:S(2)}) %collective-permute-start.11) | collective-permute-done | bytes 393248 | tf_op jit(solution)/shard_map/ppermute | solution.py:11
  346.9 3.3 collective-permute-start.12
  350.3 18.8 %collective-permute-done.12 = bf16[1,4,64,768]{3,2,1,0:T(8,128)(2,1)S(1)} collective-permute-done((bf16[1,4,64,768]{3,2,1,0:T(8,128)(2,1)S(1)}, bf16[1,4,64,768]{3,2,1,0:T(8,128)(2,1)S(1)}, u32[]{:S(2)}, u32[]{:S(2)}) %collective-permute-start.12) | collective-permute-done | bytes 393248 | tf_op jit(solution)/shard_map/ppermute | solution.py:11
  369.3 2.7 gather_fusion.2
  (149 shorter events, 65.9 us)
Async XLA Ops:
  6.5 66.2 %copy-start = (bf16[256,768]{1,0:T(8,128)(2,1)S(1)}, bf16[256,768]{1,0:T(8,128)(2,1)}, u32[]{:S(2)}) copy-start(bf16[256,768]{1,0:T(8,128)(2,1)} %param.12) | copy-start | bytes 1179652
  6.5 28.7 %copy-start.3 = (bf16[32,64,256]{2,1,0:T(8,128)(2,1)S(1)}, bf16[32,64,256]{2,1,0:T(8,128)(2,1)}, u32[]{:S(2)}) copy-start(bf16[32,64,256]{2,1,0:T(8,128)(2,1)} %param.9) | copy-start | bytes 3145732
  6.5 66.2 %all-gather.4.cloned.1.call-start = ((), (), s32[]{:S(2)}) async-start(), calls=%async_computation | async-start | bytes 1474560 | tf_op jit(solution)/shard_map/all_gather | solution.py:119
  7.3 127.0 %all-gather.6.cloned.1.call-start = ((), (), s32[]{:S(2)}) async-start(), calls=%async_computation.1 | async-start | bytes 4755456 | tf_op jit(solution)/shard_map/all_gather | solution.py:139
  9.0 27.9 %collective-permute-start.4 = (bf16[32,1,256]{2,1,0:T(2,128)(2,1)S(1)}, bf16[32,1,256]{2,1,0:T(2,128)(2,1)S(1)}, u32[]{:S(2)}, u32[]{:S(2)}) collective-permute-start(bf16[32,1,256]{2,1,0:T(2,128)(2,1)S(1)} %slice.131), channel_id=1, source_target_pairs={{0,1},{1,2},{2,3},{4,5},{5,6},{6,7},{8,9},{9,10},{10,11},{12,13},{... | collective-permute-start | bytes 49160 | tf_op jit(solution)/shard_map/ppermute | solution.py:17
  36.9 15.6 %collective-permute-start.5 = (bf16[1,65,256]{2,1,0:T(8,128)(2,1)S(1)}, bf16[1,65,256]{2,1,0:T(8,128)(2,1)S(1)}, u32[]{:S(2)}, u32[]{:S(2)}) collective-permute-start(bf16[1,65,256]{2,1,0:T(8,128)(2,1)S(1)} %fusion.51), channel_id=1, source_target_pairs={{0,4},{4,8},{8,12},{12,16},{16,20},{20,24},{24,28},{28,32},{32,36}... | collective-permute-start | bytes 99848 | tf_op jit(solution)/shard_map/ppermute | solution.py:17
  53.2 15.0 %copy-start.7 = (bf16[16,32,256]{2,1,0:T(8,128)(2,1)S(1)}, bf16[16,32,256]{2,1,0:T(8,128)(2,1)}, u32[]{:S(2)}) copy-start(bf16[16,32,256]{2,1,0:T(8,128)(2,1)} %slice.136) | copy-start | bytes 786436
  58.3 10.7 %copy-start.5 = (bf16[16,32,256]{2,1,0:T(8,128)(2,1)S(1)}, bf16[16,32,256]{2,1,0:T(8,128)(2,1)}, u32[]{:S(2)}) copy-start(bf16[16,32,256]{2,1,0:T(8,128)(2,1)} %slice.137) | copy-start | bytes 786436
  63.9 6.6 %copy-start.6 = (bf16[16,32,256]{2,1,0:T(8,128)(2,1)S(1)}, bf16[16,32,256]{2,1,0:T(8,128)(2,1)}, u32[]{:S(2)}) copy-start(bf16[16,32,256]{2,1,0:T(8,128)(2,1)} %slice.139) | copy-start | bytes 786436
  68.2 4.6 %copy-start.9 = (f32[256]{0:T(256)S(1)}, f32[256]{0:T(256)}, u32[]{:S(2)}) copy-start(f32[256]{0:T(256)} %param.11) | copy-start | bytes 3076
  76.3 57.9 %copy-start.4 = (f32[512,768]{1,0:T(8,128)}, f32[512,768]{1,0:T(8,128)S(1)}, u32[]{:S(2)}) copy-start(f32[512,768]{1,0:T(8,128)S(1)} %get-tuple-element.113) | copy-start | bytes 4718596
  148.8 8.0 %copy-start.2 = (bf16[512,2304]{1,0:T(8,128)(2,1)S(1)}, bf16[512,2304]{1,0:T(8,128)(2,1)}, u32[]{:S(2)}) copy-start(bf16[512,2304]{1,0:T(8,128)(2,1)} %gather_fusion.1) | copy-start | bytes 7077892
  151.8 5.1 %collective-permute-start.6 = (bf16[4,1,64,2304]{3,2,0,1:T(8,128)(2,1)}, bf16[4,1,64,2304]{3,2,0,1:T(8,128)(2,1)}, u32[]{:S(2)}, u32[]{:S(2)}) collective-permute-start(bf16[4,1,64,2304]{3,2,0,1:T(8,128)(2,1)} %fusion.23), channel_id=1, source_target_pairs={{0,4},{4,0},{8,12},{12,8},{16,20},{20,16},{24,28},{28,24},{32,36},... | collective-permute-start | bytes 3538952 | tf_op jit(solution)/shard_map/ppermute | solution.py:11
  159.7 29.5 %collective-permute-start.7 = (bf16[2,2,64,2304]{3,2,1,0:T(8,128)(2,1)}, bf16[2,2,64,2304]{3,2,1,0:T(8,128)(2,1)}, u32[]{:S(2)}, u32[]{:S(2)}) collective-permute-start(bf16[2,2,64,2304]{3,2,1,0:T(8,128)(2,1)} %select_bitcast_fusion.1), channel_id=1, source_target_pairs={{0,8},{4,12},{8,0},{12,4},{16,24},{20,28},{24,16},{28,20},{32,40},... | collective-permute-start | bytes 3538952 | tf_op jit(solution)/shard_map/ppermute | solution.py:11
  190.9 4.5 %copy-start.8 = (s32[16,32]{1,0:T(8,128)S(1)}, s32[16,32]{1,0:T(8,128)}, u32[]{:S(2)}) copy-start(s32[16,32]{1,0:T(8,128)} %param.14) | copy-start | bytes 6148
  192.1 56.1 %collective-permute-start.8 = (bf16[1,4,64,2304]{3,2,1,0:T(8,128)(2,1)}, bf16[1,4,64,2304]{3,2,1,0:T(8,128)(2,1)}, u32[]{:S(2)}, u32[]{:S(2)}) collective-permute-start(bf16[1,4,64,2304]{3,2,1,0:T(8,128)(2,1)} %select_bitcast_fusion), channel_id=1, source_target_pairs={{0,16},{4,20},{8,24},{12,28},{16,0},{20,4},{24,8},{28,12},{32,48},... | collective-permute-start | bytes 3538952 | tf_op jit(solution)/shard_map/ppermute | solution.py:11
  251.3 21.8 %collective-permute-start.9 = (bf16[512,1536]{1,0:T(8,128)(2,1)}, bf16[512,1536]{1,0:T(8,128)(2,1)}, u32[]{:S(2)}, u32[]{:S(2)}) collective-permute-start(bf16[512,1536]{1,0:T(8,128)(2,1)} %slice.180), channel_id=1, source_target_pairs={{0,4},{4,0},{8,12},{12,8},{16,20},{20,16},{24,28},{28,24},{32,36},... | collective-permute-start | bytes 4718600 | tf_op jit(solution)/shard_map/ppermute | solution.py:11
  253.8 3.0 collective-permute-start
  256.9 4.3 %collective-permute-start.1 = (bf16[2,2,64]{2,1,0:T(2,128)(2,1)S(1)}, bf16[2,2,64]{2,1,0:T(2,128)(2,1)S(1)}, u32[]{:S(2)}, u32[]{:S(2)}) collective-permute-start(bf16[2,2,64]{2,1,0:T(2,128)(2,1)S(1)} %bitcast.242), channel_id=1, source_target_pairs={{0,8},{4,12},{8,0},{12,4},{16,24},{20,28},{24,16},{28,20},{32,40},... | collective-permute-start | bytes 1544 | tf_op jit(solution)/shard_map/ppermute | solution.py:11
  261.2 5.2 %collective-permute-start.2 = (bf16[1,4,64]{2,1,0:T(4,128)(2,1)S(1)}, bf16[1,4,64]{2,1,0:T(4,128)(2,1)S(1)}, u32[]{:S(2)}, u32[]{:S(2)}) collective-permute-start(bf16[1,4,64]{2,1,0:T(4,128)(2,1)S(1)} %select_bitcast_fusion.4), channel_id=1, source_target_pairs={{0,16},{4,20},{8,24},{12,28},{16,0},{20,4},{24,8},{28,12},{32,48},... | collective-permute-start | bytes 1544 | tf_op jit(solution)/shard_map/ppermute | solution.py:11
  266.6 5.3 %collective-permute-start.3 = (bf16[512]{0:T(512)(128)(2,1)S(1)}, bf16[512]{0:T(512)(128)(2,1)S(1)}, u32[]{:S(2)}, u32[]{:S(2)}) collective-permute-start(bf16[512]{0:T(512)(128)(2,1)S(1)} %reshape_reshape.30), channel_id=1, source_target_pairs={{0,4},{4,0},{8,12},{12,8},{16,20},{20,16},{24,28},{28,24},{32,36},... | collective-permute-start | bytes 3080 | tf_op jit(solution)/shard_map/ppermute | solution.py:11
  330.4 3.8 %collective-permute-start.10 = (bf16[4,1,64,768]{3,2,0,1:T(8,128)(2,1)}, bf16[4,1,64,768]{3,2,0,1:T(8,128)(2,1)S(1)}, u32[]{:S(2)}, u32[]{:S(2)}) collective-permute-start(bf16[4,1,64,768]{3,2,0,1:T(8,128)(2,1)} %bitcast.56), channel_id=1, source_target_pairs={{0,4},{4,0},{8,12},{12,8},{16,20},{20,16},{24,28},{28,24},{32,36},... | collective-permute-start | bytes 1179656 | tf_op jit(solution)/shard_map/ppermute | solution.py:11
  334.4 12.3 %collective-permute-start.11 = (bf16[2,2,64,768]{3,2,1,0:T(8,128)(2,1)S(1)}, bf16[2,2,64,768]{3,2,1,0:T(8,128)(2,1)S(1)}, u32[]{:S(2)}, u32[]{:S(2)}) collective-permute-start(bf16[2,2,64,768]{3,2,1,0:T(8,128)(2,1)S(1)} %select_bitcast_fusion.3), channel_id=1, source_target_pairs={{0,8},{4,12},{8,0},{12,4},{16,24},{20,28},{24,16},{28,20},{32,40},... | collective-permute-start | bytes 1179656 | tf_op jit(solution)/shard_map/ppermute | solution.py:11
  346.9 22.2 %collective-permute-start.12 = (bf16[1,4,64,768]{3,2,1,0:T(8,128)(2,1)S(1)}, bf16[1,4,64,768]{3,2,1,0:T(8,128)(2,1)S(1)}, u32[]{:S(2)}, u32[]{:S(2)}) collective-permute-start(bf16[1,4,64,768]{3,2,1,0:T(8,128)(2,1)S(1)} %select_bitcast_fusion.2), channel_id=1, source_target_pairs={{0,16},{4,20},{8,24},{12,28},{16,0},{20,4},{24,8},{28,12},{32,48},... | collective-permute-start | bytes 1179656 | tf_op jit(solution)/shard_map/ppermute | solution.py:11
  369.2 2.7 copy-start.1
Sparse Core Ops, SparseCore 0:
  9.5 34.2 all-gather.3
  46.9 87.2 all-gather.5
where the time goes:
time: 381 us; the launch traced here: 379 us
  waiting for transfers between devices  174 us (46%)
  local copies, waits for them, and re-layouts  81.4 us (21%)
  matrix products  41.6 us (11%)
  starting transfers between devices  38 us (10%)
  other arithmetic  29.8 us (8%)
  between operations  13.9 us (4%)
    ppermute x11, waiting for transfers between devices, partner(): lax.ppermute(array, axis, [(i, i ^ 1 << apart) for i in range(lax.axis_si...  115 us
    all_gather x1, waiting for transfers between devices, local(): lax.all_gather(qkv_weight, 'row', axis=0, tiled=True)  57.6 us
    slice x9, local copies, waits for them, and re-layouts, local(): padded[row_tap:row_tap + in_rows - 1:2, col_tap:col_tap + in_cols - 1:2, :]  38.1 us
    ppermute x11, starting transfers between devices, partner(): lax.ppermute(array, axis, [(i, i ^ 1 << apart) for i in range(lax.axis_si...  29.2 us
    dot_general x12, matrix products, one_head(): jnp.einsum('qd,kd->qk', query_head, key_head, preferred_element_type=jnp....  17.8 us
    dot_general x12, matrix products, one_head(): jnp.dot(weights.astype(jnp.bfloat16), value_head, preferred_element_type=...  15.8 us
    unnamed x30, local copies, waits for them, and re-layouts  14.7 us
    ppermute x2, starting transfers between devices, shifted(): return lax.ppermute(array, axis, pairs)  8.79 us
  transfers between devices with their start and end apart: 15, of which 11 were waited for; matrix products, arithmetic and copies ran while one was open for 17% of the time, Pallas kernels for 0%

commit v1 on v0

--- a/solution.py
+++ b/solution.py
@@ -5,6 +5,19 @@
 
 HD = 64
 DILATION_STEP = 4
+
+
+def _press_boxes(content, chip_axis, ndim_at):
+    after = jnp.concatenate(
+        jax.lax.all_to_all(
+            jnp.stack([content for _ in range(jax.lax.psum(1, chip_axis))]),
+            axis_name=chip_axis,
+            split_axis=0,
+            concat_axis=0,
+        ),
+        ndim_at,
+    )
+    return after
 
 
 def partner(array, axis, apart):
@@ -136,9 +149,7 @@
     )
     tissue_flag = tissue.reshape(token_count).astype(jnp.bfloat16)
     flag_out = tissue_flag[inverse].reshape(owner_labels, capacity)
-    qkv_local = fold_rows(tokens_bf, lax.all_gather(qkv_weight, "row", axis=0, tiled=True)).astype(
-        jnp.bfloat16
-    )
+    qkv_local = fold_rows(tokens_bf, _press_boxes(qkv_weight, "row", 0)).astype(jnp.bfloat16)
     arrived, arrived_flag = route_sender(
         qkv_local[inverse].reshape(owner_labels, capacity, 3 * model_width), flag_out
     )

time: 381 us -> 409 us (1.073)
  the two profiles are of different devices: /device:TPU:1 before, /device:TPU:63 now
where the time goes in v1:
time: 409 us; the launch traced here: 408 us
  waiting for transfers between devices  199 us (49%)
  local copies, waits for them, and re-layouts  73 us (18%)
  starting transfers between devices  50.6 us (12%)
  matrix products  41.6 us (10%)
  other arithmetic  29.1 us (7%)
  between operations  14 us (3%)
    ppermute x11, waiting for transfers between devices, partner(): lax.ppermute(array, axis, [(i, i ^ 1 << apart) for i in range(lax.axis_si...  117 us
    ppermute x2, waiting for transfers between devices, shifted(): return lax.ppermute(array, axis, pairs)  81.9 us
    slice x9, local copies, waits for them, and re-layouts, local(): padded[row_tap:row_tap + in_rows - 1:2, col_tap:col_tap + in_cols - 1:2, :]  28 us
    ppermute x11, starting transfers between devices, partner(): lax.ppermute(array, axis, [(i, i ^ 1 << apart) for i in range(lax.axis_si...  27.7 us
    all_to_all x1, starting transfers between devices, _press_boxes(): jax.lax.all_to_all(jnp.stack([content for _ in range(jax.lax.psum(1, chip...  18.2 us
    dot_general x12, matrix products, one_head(): jnp.einsum('qd,kd->qk', query_head, key_head, preferred_element_type=jnp....  17.8 us
    dot_general x12, matrix products, one_head(): jnp.dot(weights.astype(jnp.bfloat16), value_head, preferred_element_type=...  15.8 us
    unnamed x31, local copies, waits for them, and re-layouts  8.91 us
  transfers between devices with their start and end apart: 15, of which 11 were waited for; matrix products, arithmetic and copies ran while one was open for 13% of the time, Pallas kernels for 0%

profile of v1, /device:TPU:63, one launch (start us, length us, event | category | flops | bytes accessed | tf_op | source)
XLA Modules:
  0.0 407.6 jit_solution(6063986819426571524)
XLA Ops:
  6.5 3.3 stack.65
  9.8 18.2 %all-to-all-start = ((bf16[128,6,2304]{2,1,0:T(8,128)(2,1)}), bf16[128,6,2304]{2,1,0:T(8,128)(2,1)}, u32[]{:S(2)}, u32[]{:S(2)}) async-start(bf16[128,6,2304]{2,1,0:T(8,128)(2,1)} %stack.65), calls=%async_computation | async-start | bytes 9437184 | tf_op jit(solution)/shard_map/all_to_all | solution.py:12
  31.5 2.4 scatter_custom_fusion
  33.9 5.1 %slice.137 = bf16[16,32,256]{2,1,0:T(8,128)(2,1)} slice(bf16[32,64,256]{2,1,0:T(8,128)(2,1)S(1)} %copy-done.3), slice={[0:31:2], [0:63:2], [0:256:1]} | slice | bytes 524288 | tf_op jit(solution)/shard_map/slice | solution.py:127
  41.2 3.4 collective-permute-start.5
  45.2 5.0 %slice.136 = bf16[16,32,256]{2,1,0:T(8,128)(2,1)} slice(bf16[32,65,256]{2,1,0:T(8,128)(2,1)S(1)} %pad_maximum_fusion.2), slice={[0:31:2], [0:63:2], [0:256:1]} | slice | bytes 524288 | tf_op jit(solution)/shard_map/slice | solution.py:127
  50.2 5.0 %slice.139 = bf16[16,32,256]{2,1,0:T(8,128)(2,1)} slice(bf16[32,65,256]{2,1,0:T(8,128)(2,1)S(1)} %pad_maximum_fusion.2), slice={[1:32:2], [0:63:2], [0:256:1]} | slice | bytes 524288 | tf_op jit(solution)/shard_map/slice | solution.py:127
  55.3 81.9 %collective-permute-done.5 = bf16[1,65,256]{2,1,0:T(8,128)(2,1)S(1)} collective-permute-done((bf16[1,65,256]{2,1,0:T(8,128)(2,1)S(1)}, bf16[1,65,256]{2,1,0:T(8,128)(2,1)S(1)}, u32[]{:S(2)}, u32[]{:S(2)}) %collective-permute-start.5) | collective-permute-done | bytes 33312 | tf_op jit(solution)/shard_map/ppermute | solution.py:30
  137.9 5.1 %slice.133 = bf16[16,32,256]{2,1,0:T(8,128)(2,1)} slice(bf16[33,65,256]{2,1,0:T(8,128)(2,1)S(1)} %maximum_maximum_fusion), slice={[0:31:2], [0:63:2], [0:256:1]} | slice | bytes 524288 | tf_op jit(solution)/shard_map/slice | solution.py:127
  142.9 5.0 %slice.134 = bf16[16,32,256]{2,1,0:T(8,128)(2,1)} slice(bf16[33,65,256]{2,1,0:T(8,128)(2,1)S(1)} %maximum_maximum_fusion), slice={[0:31:2], [1:64:2], [0:256:1]} | slice | bytes 524288 | tf_op jit(solution)/shard_map/slice | solution.py:127
  148.6 1.8 constant_dynamic-update-slice_fusion.8
  150.3 1.7 constant_dynamic-update-slice_fusion.7
  157.4 3.5 fusion.67
  162.1 6.6 %reshape.535 = bf16[768,2304]{1,0:T(8,128)(2,1)} reshape(bf16[128,6,2304]{2,1,0:T(8,128)(2,1)} %all-to-all-done) | data formatting | bytes 7077888 | tf_op jit(solution)/shard_map/reshape | solution.py:11
  168.7 4.5 %convolution_convert_fusion = bf16[512,2304]{1,0:T(8,128)(2,1)S(1)} fusion(bf16[768,2304]{1,0:T(8,128)(2,1)} %reshape.535, f32[512,768]{1,0:T(8,128)} %copy-done.4, f32[512]{0:T(512)S(1)} %add_rsqrt_fusion, f32[512]{0:T(512)S(1)} %broadcast_multiply_fusion.1), kind=kOutput, calls=%fused_computation.28 | convolution fusion | flops 1814298624 | bytes 7475200 | tf_op jit(solution)/shard_map/dot_general | solution.py:40
  173.2 3.4 gather_fusion.1
  176.6 2.9 fusion.23
  179.6 1.9 collective-permute-start.6
  181.5 3.1 collective-permute-done.6
  187.5 4.1 %collective-permute-start.7 = (bf16[2,2,64,2304]{3,2,1,0:T(8,128)(2,1)}, bf16[2,2,64,2304]{3,2,1,0:T(8,128)(2,1)}, u32[]{:S(2)}, u32[]{:S(2)}) collective-permute-start(bf16[2,2,64,2304]{3,2,1,0:T(8,128)(2,1)} %select_bitcast_fusion.1), channel_id=1, source_target_pairs={{0,8},{4,12},{8,0},{12,4},{16,24},{20,28},{24,16},{28,20},{32,40},... | collective-permute-start | bytes 3538952 | tf_op jit(solution)/shard_map/ppermute | solution.py:24
  191.6 26.3 %collective-permute-done.7 = bf16[2,2,64,2304]{3,2,1,0:T(8,128)(2,1)} collective-permute-done((bf16[2,2,64,2304]{3,2,1,0:T(8,128)(2,1)}, bf16[2,2,64,2304]{3,2,1,0:T(8,128)(2,1)}, u32[]{:S(2)}, u32[]{:S(2)}) %collective-permute-start.7) | collective-permute-done | bytes 1179680 | tf_op jit(solution)/shard_map/ppermute | solution.py:24
  220.9 2.1 collective-permute-start.8
  223.1 3.5 gather_fusion
  226.7 49.6 %collective-permute-done.8 = bf16[1,4,64,2304]{3,2,1,0:T(8,128)(2,1)} collective-permute-done((bf16[1,4,64,2304]{3,2,1,0:T(8,128)(2,1)}, bf16[1,4,64,2304]{3,2,1,0:T(8,128)(2,1)}, u32[]{:S(2)}, u32[]{:S(2)}) %collective-permute-start.8) | collective-permute-done | bytes 1179680 | tf_op jit(solution)/shard_map/ppermute | solution.py:24
  279.2 3.3 collective-permute-start.9
  282.6 1.9 collective-permute-start
  285.6 1.9 collective-permute-start.1
  287.5 2.4 collective-permute-done.1
  290.0 1.9 collective-permute-start.2
  291.9 3.3 collective-permute-done.2
  295.3 4.5 %collective-permute-start.3 = (bf16[512]{0:T(512)(128)(2,1)S(1)}, bf16[512]{0:T(512)(128)(2,1)S(1)}, u32[]{:S(2)}, u32[]{:S(2)}) collective-permute-start(bf16[512]{0:T(512)(128)(2,1)S(1)} %reshape_reshape.30), channel_id=1, source_target_pairs={{0,4},{4,0},{8,12},{12,8},{16,20},{20,16},{24,28},{28,24},{32,36},... | collective-permute-start | bytes 3080 | tf_op jit(solution)/shard_map/ppermute | solution.py:24
  301.8 2.0 pad_maximum_fusion.3
  303.9 1.7 copy.108
  306.3 41.7 %while.10 = (s32[]{:T(128)}, f32[12,512,64]{1,2,0:T(8,128)}, pred[1,1024]{1,0:T(4,128)(4,1)S(1)}, bf16[12,512,64]{1,2,0:T(8,128)(2,1)}, bf16[12,1024,64]{1,2,0:T...) while((s32[]{:T(128)}, f32[12,512,64]{1,2,0:T(8,128)}, ...), condition=%wide.region_9.10_spmd, body=%wide.region_6.9_spmd.sunk | while | flops 141065216 | bytes 6767702 | solution.py:106
  306.3 1.5 fusion.79
  313.3 1.5 fusion.79
  316.8 1.5 fusion.79
  320.2 1.5 fusion.79
  327.2 1.5 fusion.79
  348.0 3.6 reshape.539
  352.7 3.7 broadcast_select_fusion.1
  356.4 2.7 copy.114
  359.1 2.2 collective-permute-start.10
  363.1 1.9 collective-permute-start.11
  365.0 10.3 %collective-permute-done.11 = bf16[2,2,64,768]{3,2,1,0:T(8,128)(2,1)S(1)} collective-permute-done((bf16[2,2,64,768]{3,2,1,0:T(8,128)(2,1)S(1)}, bf16[2,2,64,768]{3,2,1,0:T(8,128)(2,1)S(1)}, u32[]{:S(2)}, u32[]{:S(2)}) %collective-permute-start.11) | collective-permute-done | bytes 393248 | tf_op jit(solution)/shard_map/ppermute | solution.py:24
  375.7 1.9 collective-permute-start.12
  377.6 20.3 %collective-permute-done.12 = bf16[1,4,64,768]{3,2,1,0:T(8,128)(2,1)S(1)} collective-permute-done((bf16[1,4,64,768]{3,2,1,0:T(8,128)(2,1)S(1)}, bf16[1,4,64,768]{3,2,1,0:T(8,128)(2,1)S(1)}, u32[]{:S(2)}, u32[]{:S(2)}) %collective-permute-start.12) | collective-permute-done | bytes 393248 | tf_op jit(solution)/shard_map/ppermute | solution.py:24
  398.0 2.7 gather_fusion.2
  (151 shorter events, 64.3 us)
Async XLA Ops:
  6.5 150.9 %copy-start = (bf16[256,768]{1,0:T(8,128)(2,1)S(1)}, bf16[256,768]{1,0:T(8,128)(2,1)}, u32[]{:S(2)}) copy-start(bf16[256,768]{1,0:T(8,128)(2,1)} %param.12) | copy-start | bytes 1179652
  9.8 18.2 %copy-start.3 = (bf16[32,64,256]{2,1,0:T(8,128)(2,1)S(1)}, bf16[32,64,256]{2,1,0:T(8,128)(2,1)}, u32[]{:S(2)}) copy-start(bf16[32,64,256]{2,1,0:T(8,128)(2,1)} %param.9) | copy-start | bytes 3145732
  9.8 19.6 %copy-start.8 = (s32[16,32]{1,0:T(8,128)S(1)}, s32[16,32]{1,0:T(8,128)}, u32[]{:S(2)}) copy-start(s32[16,32]{1,0:T(8,128)} %param.15) | copy-start | bytes 6148
  9.8 151.4 %all-to-all-start = ((bf16[128,6,2304]{2,1,0:T(8,128)(2,1)}), bf16[128,6,2304]{2,1,0:T(8,128)(2,1)}, u32[]{:S(2)}, u32[]{:S(2)}) async-start(bf16[128,6,2304]{2,1,0:T(8,128)(2,1)} %stack.65), calls=%async_computation | async-start | bytes 9437184 | tf_op jit(solution)/shard_map/all_to_all | solution.py:12
  28.0 129.4 %all-gather.2.cloned.1.call-start = ((), (), s32[]{:S(2)}) async-start(), calls=%async_computation.1 | async-start | bytes 1474560 | tf_op jit(solution)/shard_map/all_gather | solution.py:132
  28.1 13.0 %collective-permute-start.4 = (bf16[32,1,256]{2,1,0:T(2,128)(2,1)S(1)}, bf16[32,1,256]{2,1,0:T(2,128)(2,1)S(1)}, u32[]{:S(2)}, u32[]{:S(2)}) collective-permute-start(bf16[32,1,256]{2,1,0:T(2,128)(2,1)S(1)} %slice.131), channel_id=1, source_target_pairs={{0,1},{1,2},{2,3},{4,5},{5,6},{6,7},{8,9},{9,10},{10,11},{12,13},{... | collective-permute-start | bytes 49160 | tf_op jit(solution)/shard_map/ppermute | solution.py:30
  41.2 96.0 %collective-permute-start.5 = (bf16[1,65,256]{2,1,0:T(8,128)(2,1)S(1)}, bf16[1,65,256]{2,1,0:T(8,128)(2,1)S(1)}, u32[]{:S(2)}, u32[]{:S(2)}) collective-permute-start(bf16[1,65,256]{2,1,0:T(8,128)(2,1)S(1)} %fusion.51), channel_id=1, source_target_pairs={{0,4},{4,8},{8,12},{12,16},{16,20},{20,24},{24,28},{28,32},{32,36}... | collective-permute-start | bytes 99848 | tf_op jit(solution)/shard_map/ppermute | solution.py:30
  137.8 15.0 %copy-start.7 = (bf16[16,32,256]{2,1,0:T(8,128)(2,1)S(1)}, bf16[16,32,256]{2,1,0:T(8,128)(2,1)}, u32[]{:S(2)}) copy-start(bf16[16,32,256]{2,1,0:T(8,128)(2,1)} %slice.136) | copy-start | bytes 786436
  142.9 10.7 %copy-start.5 = (bf16[16,32,256]{2,1,0:T(8,128)(2,1)S(1)}, bf16[16,32,256]{2,1,0:T(8,128)(2,1)}, u32[]{:S(2)}) copy-start(bf16[16,32,256]{2,1,0:T(8,128)(2,1)} %slice.137) | copy-start | bytes 786436
  148.6 6.5 %copy-start.6 = (bf16[16,32,256]{2,1,0:T(8,128)(2,1)S(1)}, bf16[16,32,256]{2,1,0:T(8,128)(2,1)}, u32[]{:S(2)}) copy-start(bf16[16,32,256]{2,1,0:T(8,128)(2,1)} %slice.139) | copy-start | bytes 786436
  152.9 4.5 %copy-start.10 = (f32[256]{0:T(256)S(1)}, f32[256]{0:T(256)}, u32[]{:S(2)}) copy-start(f32[256]{0:T(256)} %param.11) | copy-start | bytes 3076
  160.9 1.2 copy-start.4
  176.6 8.0 %copy-start.2 = (bf16[512,2304]{1,0:T(8,128)(2,1)S(1)}, bf16[512,2304]{1,0:T(8,128)(2,1)}, u32[]{:S(2)}) copy-start(bf16[512,2304]{1,0:T(8,128)(2,1)} %gather_fusion.1) | copy-start | bytes 7077892
  179.6 5.1 %collective-permute-start.6 = (bf16[4,1,64,2304]{3,2,0,1:T(8,128)(2,1)}, bf16[4,1,64,2304]{3,2,0,1:T(8,128)(2,1)}, u32[]{:S(2)}, u32[]{:S(2)}) collective-permute-start(bf16[4,1,64,2304]{3,2,0,1:T(8,128)(2,1)} %fusion.23), channel_id=1, source_target_pairs={{0,4},{4,0},{8,12},{12,8},{16,20},{20,16},{24,28},{28,24},{32,36},... | collective-permute-start | bytes 3538952 | tf_op jit(solution)/shard_map/ppermute | solution.py:24
  187.5 30.4 %collective-permute-start.7 = (bf16[2,2,64,2304]{3,2,1,0:T(8,128)(2,1)}, bf16[2,2,64,2304]{3,2,1,0:T(8,128)(2,1)}, u32[]{:S(2)}, u32[]{:S(2)}) collective-permute-start(bf16[2,2,64,2304]{3,2,1,0:T(8,128)(2,1)} %select_bitcast_fusion.1), channel_id=1, source_target_pairs={{0,8},{4,12},{8,0},{12,4},{16,24},{20,28},{24,16},{28,20},{32,40},... | collective-permute-start | bytes 3538952 | tf_op jit(solution)/shard_map/ppermute | solution.py:24
  219.7 3.3 copy-start.9
  220.9 55.4 %collective-permute-start.8 = (bf16[1,4,64,2304]{3,2,1,0:T(8,128)(2,1)}, bf16[1,4,64,2304]{3,2,1,0:T(8,128)(2,1)}, u32[]{:S(2)}, u32[]{:S(2)}) collective-permute-start(bf16[1,4,64,2304]{3,2,1,0:T(8,128)(2,1)} %select_bitcast_fusion), channel_id=1, source_target_pairs={{0,16},{4,20},{8,24},{12,28},{16,0},{20,4},{24,8},{28,12},{32,48},... | collective-permute-start | bytes 3538952 | tf_op jit(solution)/shard_map/ppermute | solution.py:24
  279.2 22.6 %collective-permute-start.9 = (bf16[512,1536]{1,0:T(8,128)(2,1)}, bf16[512,1536]{1,0:T(8,128)(2,1)}, u32[]{:S(2)}, u32[]{:S(2)}) collective-permute-start(bf16[512,1536]{1,0:T(8,128)(2,1)} %slice.180), channel_id=1, source_target_pairs={{0,4},{4,0},{8,12},{12,8},{16,20},{20,16},{24,28},{28,24},{32,36},... | collective-permute-start | bytes 4718600 | tf_op jit(solution)/shard_map/ppermute | solution.py:24
  282.6 3.0 collective-permute-start
  285.6 4.3 %collective-permute-start.1 = (bf16[2,2,64]{2,1,0:T(2,128)(2,1)S(1)}, bf16[2,2,64]{2,1,0:T(2,128)(2,1)S(1)}, u32[]{:S(2)}, u32[]{:S(2)}) collective-permute-start(bf16[2,2,64]{2,1,0:T(2,128)(2,1)S(1)} %bitcast.240), channel_id=1, source_target_pairs={{0,8},{4,12},{8,0},{12,4},{16,24},{20,28},{24,16},{28,20},{32,40},... | collective-permute-start | bytes 1544 | tf_op jit(solution)/shard_map/ppermute | solution.py:24
  290.0 5.2 %collective-permute-start.2 = (bf16[1,4,64]{2,1,0:T(4,128)(2,1)S(1)}, bf16[1,4,64]{2,1,0:T(4,128)(2,1)S(1)}, u32[]{:S(2)}, u32[]{:S(2)}) collective-permute-start(bf16[1,4,64]{2,1,0:T(4,128)(2,1)S(1)} %select_bitcast_fusion.4), channel_id=1, source_target_pairs={{0,16},{4,20},{8,24},{12,28},{16,0},{20,4},{24,8},{28,12},{32,48},... | collective-permute-start | bytes 1544 | tf_op jit(solution)/shard_map/ppermute | solution.py:24
  295.3 5.3 %collective-permute-start.3 = (bf16[512]{0:T(512)(128)(2,1)S(1)}, bf16[512]{0:T(512)(128)(2,1)S(1)}, u32[]{:S(2)}, u32[]{:S(2)}) collective-permute-start(bf16[512]{0:T(512)(128)(2,1)S(1)} %reshape_reshape.30), channel_id=1, source_target_pairs={{0,4},{4,0},{8,12},{12,8},{16,20},{20,16},{24,28},{28,24},{32,36},... | collective-permute-start | bytes 3080 | tf_op jit(solution)/shard_map/ppermute | solution.py:24
  359.1 3.8 collective-permute-start.10
  363.1 12.3 %collective-permute-start.11 = (bf16[2,2,64,768]{3,2,1,0:T(8,128)(2,1)S(1)}, bf16[2,2,64,768]{3,2,1,0:T(8,128)(2,1)S(1)}, u32[]{:S(2)}, u32[]{:S(2)}) collective-permute-start(bf16[2,2,64,768]{3,2,1,0:T(8,128)(2,1)S(1)} %select_bitcast_fusion.3), channel_id=1, source_target_pairs={{0,8},{4,12},{8,0},{12,4},{16,24},{20,28},{24,16},{28,20},{32,40},... | collective-permute-start | bytes 1179656 | tf_op jit(solution)/shard_map/ppermute | solution.py:24
  375.7 22.2 %collective-permute-start.12 = (bf16[1,4,64,768]{3,2,1,0:T(8,128)(2,1)S(1)}, bf16[1,4,64,768]{3,2,1,0:T(8,128)(2,1)S(1)}, u32[]{:S(2)}, u32[]{:S(2)}) collective-permute-start(bf16[1,4,64,768]{3,2,1,0:T(8,128)(2,1)S(1)} %select_bitcast_fusion.2), channel_id=1, source_target_pairs={{0,16},{4,20},{8,24},{12,28},{16,0},{20,4},{24,8},{28,12},{32,48},... | collective-permute-start | bytes 1179656 | tf_op jit(solution)/shard_map/ppermute | solution.py:24
  398.0 2.7 copy-start.1
Sparse Core Ops, SparseCore 0:
  31.0 28.2 all-gather.1
